TPU v7x, 32 devices: a whole 2x2x4 slice. The times are simulated.
32 devices in a mesh: segment: 4 (over y, x), dom: 8 (over z, core).
Axes of the slice: x: 2, y: 2, z: 4, core: 2. Of those that a mesh axis runs over, the one named last changes fastest.
Arguments:
- features: bfloat16 [4, 4096, 512], P(None, 'dom'), may hold values from -6 to 6
- send_rows: int32 [4, 8, 8, 128], P(None, 'dom'), may hold values from 0 to 511
- send_len: int32 [4, 8, 8], P(None, 'dom'), may hold values from 0 to 128, as said below
- tile_src: int32 [4, 32, 4], P(None, 'dom'), may hold values from 0 to 11
- tile_count: int32 [4, 32], P(None, 'dom'), may hold values from 1 to 4, as said below
- tile_val: bfloat16 [4, 32, 4, 128, 128], P(None, 'dom'), may hold values from -0.25 to 0.25
- w_self: bfloat16 [4, 512, 512], P('segment'), may hold values from -0.25 to 0.25
- w_neigh: bfloat16 [4, 512, 512], P('segment'), may hold values from -0.25 to 0.25
- gain: bfloat16 [4, 512], P('segment'), may hold values from 0.25 to 1.75
- bias: bfloat16 [4, 512], P('segment'), may hold values from -3 to 3
Outputs:
- acts: bfloat16 [4, 4, 4096, 512], P('segment', None, 'dom')
Inputs may be any that keep to these rules, and one draw needn't show every extreme that they name: `send_len`: A partition sends nothing to itself; in every span each partition sends a full block of 128 rows to one other partition. `tile_count`: in every span one partition has 4 live tiles in each of its blocks.
All inputs are finite; a program needn't handle non-finite values.
Results may differ from a plain program's by a relative error of at most 0.0065.
Values may be sent and summed in bfloat16 or wider, within the bound.
No kernel may reach another device: no remote copies, remote signals or barrier semaphores. Data moves between devices by JAX's collectives and lax.ppermute only.
A program may use at most 64 MiB of HBM per device.

v0:
```python
import jax
import jax.numpy as jnp
from jax import lax
from jax.sharding import PartitionSpec as P

norm_eps = 1e-05


def select_span(array_in, span_id):
    return lax.dynamic_index_in_dim(array_in, span_id, 0, keepdims=False)


def sage_layer(inputs, span_id, graph, w_one, w_two, gain_one, bias_one):
    rows_all, lens_all, src_all, count_all, vals_all = graph
    send_list = select_span(rows_all, span_id)[0]
    send_count = select_span(lens_all, span_id)[0]
    tile_index = select_span(src_all, span_id)
    tile_total = select_span(count_all, span_id)
    tile_vals = select_span(vals_all, span_id)
    peer_count, tile_rows = send_list.shape
    feat_width = inputs.shape[1]
    block_count, tile_depth = tile_index.shape
    picked = jnp.take(inputs, send_list.reshape(-1), axis=0).reshape(
        peer_count, tile_rows, feat_width
    )
    row_live = lax.broadcasted_iota(jnp.int32, (peer_count, tile_rows), 1) < send_count[:, None]
    outgoing = jnp.where(row_live[:, :, None], picked, jnp.zeros_like(picked))
    incoming = lax.all_to_all(outgoing, "dom", split_axis=0, concat_axis=0, tiled=True)
    sources = jnp.concatenate(
        [inputs.reshape(block_count, tile_rows, feat_width), incoming], axis=0
    )
    tile_live = lax.broadcasted_iota(jnp.int32, (block_count, tile_depth), 1) < tile_total[:, None]

    def block_sum(packed):
        block_index, block_vals, block_live = packed
        chosen = jnp.take(sources, block_index, axis=0)
        masked = jnp.where(block_live[:, None, None], block_vals, jnp.zeros_like(block_vals))
        return jnp.einsum("kij,kjd->id", masked, chosen, preferred_element_type=jnp.float32)

    summed = lax.map(block_sum, (tile_index, tile_vals, tile_live))
    gathered = summed.reshape(block_count * tile_rows, feat_width).astype(jnp.bfloat16)
    mixed = jnp.dot(inputs, w_one, preferred_element_type=jnp.float32) + jnp.dot(
        gathered, w_two, preferred_element_type=jnp.float32
    )
    center = mixed - jnp.mean(mixed, axis=1, keepdims=True)
    spread = jnp.mean(center * center, axis=1, keepdims=True)
    scaled = center * lax.rsqrt(spread + norm_eps) * gain_one.astype(jnp.float32) + bias_one.astype(
        jnp.float32
    )
    return jnp.maximum(scaled, 0.0).astype(jnp.bfloat16)


def per_device(
    features, send_rows, send_len, tile_src, tile_count, tile_val, w_self, w_neigh, gain, bias
):
    segments = lax.axis_size("segment")
    segment_id = lax.axis_index("segment")
    span_total, node_rows, feat_width = features.shape
    graph = (send_rows, send_len, tile_src, tile_count, tile_val)
    every_self, every_neigh, every_gain, every_bias = (
        lax.all_gather(w_self, "segment", axis=0, tiled=True),
        lax.all_gather(w_neigh, "segment", axis=0, tiled=True),
        lax.all_gather(gain, "segment", axis=0, tiled=True),
        lax.all_gather(bias, "segment", axis=0, tiled=True),
    )
    span_group = span_total // segments
    layers = every_self.shape[0]
    span_id = segment_id * span_group + 0
    hidden = select_span(features, span_id)
    outputs = []
    for layer_id in range(layers):
        hidden = sage_layer(
            hidden,
            span_id,
            graph,
            every_self[layer_id],
            every_neigh[layer_id],
            every_gain[layer_id],
            every_bias[layer_id],
        )
        outputs.append(hidden)
    finished = [jnp.stack(outputs)]
    dealt_out = jnp.stack(finished, axis=1)
    return lax.all_to_all(dealt_out, "segment", split_axis=0, concat_axis=1, tiled=True)


def solution(mesh):
    in_specs = (
        P(None, "dom", None),
        P(None, "dom", None, None),
        P(None, "dom", None),
        P(None, "dom", None),
        P(None, "dom"),
        P(None, "dom", None, None, None),
        P("segment", None, None),
        P("segment", None, None),
        P("segment", None),
        P("segment", None),
    )
    out_specs = P("segment", None, "dom", None)
    return jax.shard_map(
        per_device, mesh=mesh, in_specs=in_specs, out_specs=out_specs, check_vma=False
    )
```

profile of v0, /device:TPU:0, one launch (start us, length us, event | category | flops | bytes accessed | tf_op | source)
XLA Modules:
  0.0 296.5 jit_solution(8535459585677246511)
XLA Ops:
  8.2 5.1 %gather_fusion.4 = bf16[1024,512]{1,0:T(8,128)(2,1)} fusion(bf16[512,512]{1,0:T(8,128)(2,1)S(1)} %fusion.67, s32[1024]{0:T(1024)S(1)} %fusion.49), kind=kCustom, calls=%fused_computation.clone | custom fusion | bytes 2101248 | tf_op jit(solution)/shard_map/jit(_take)/gather | solution.py:23
  14.7 1.4 broadcast_select_fusion.3
  17.3 6.5 %all-to-all-start = ((bf16[8,128,512]{2,1,0:T(8,128)(2,1)}), bf16[8,128,512]{2,1,0:T(8,128)(2,1)}, u32[]{:S(2)}, u32[]{:S(2)}) async-start(bf16[8,128,512]{2,1,0:T(8,128)(2,1)} %broadcast_select_fusion.7), calls=%async_computation | async-start | bytes 2097152 | tf_op jit(solution)/shard_map/all_to_all | solution.py:28
  24.5 8.1 %all-gather = bf16[4,1,512]{2,1,0:T(2,128)(2,1)S(1)} all-gather(bf16[1,1,512]{2,1,0:T(2,128)(2,1)S(1)} %bitcast.203), channel_id=1, replica_groups=mesh['segment'=4,'dom'=8] {'segment'}, dimensions={0}, use_global_device_ids=true | all-gather | bytes 5120 | tf_op jit(solution)/shard_map/all_gather | solution.py:63
  34.1 8.3 %all-gather.1 = bf16[4,1,512]{2,1,0:T(2,128)(2,1)S(1)} all-gather(bf16[1,1,512]{2,1,0:T(2,128)(2,1)S(1)} %bitcast.204), channel_id=1, replica_groups=mesh['segment'=4,'dom'=8] {'segment'}, dimensions={0}, use_global_device_ids=true | all-gather | bytes 5120 | tf_op jit(solution)/shard_map/all_gather | solution.py:64
  42.4 1.9 dynamic-slice_bitcast_fusion.4
  44.3 6.1 %all-to-all-done = bf16[8,128,512]{2,1,0:T(8,128)(2,1)} async-done(((bf16[8,128,512]{2,1,0:T(8,128)(2,1)}), bf16[8,128,512]{2,1,0:T(8,128)(2,1)}, u32[]{:S(2)}, u32[]{:S(2)}) %all-to-all-start) | async-done | bytes 1048608 | tf_op jit(solution)/shard_map/all_to_all | solution.py:28
  50.4 2.5 pad_maximum_fusion
  53.8 15.7 %while.40 = (s32[]{:T(128)}, bf16[4,128,512]{2,1,0:T(8,128)(2,1)}, pred[4,4]{1,0:T(4,128)(4,1)S(1)}, bf16[4,4,128,128]{3,2,1,0:T(8,128)(2,1)}, s32[4,4]{1,0:T(4,...) while((s32[]{:T(128)}, bf16[4,128,512]{2,1,0:T(8,128)(2,1)}, pred[4,4]{1,0:T(4,128)(4,1)S(1)}, ...), condition=%wide.region_1.4_spmd, body=%wide.region_0.3_spmd.sunk | while | flops 67437592 | bytes 1971369 | solution.py:40
  53.8 2.0 gather_fusion
  55.8 1.9 fusion.77
  57.8 2.0 gather_fusion
  59.8 1.9 fusion.77
  61.7 2.0 gather_fusion
  63.7 1.9 fusion.77
  65.6 2.0 gather_fusion
  67.6 1.9 fusion.77
  69.5 2.5 fusion.48
  72.0 12.2 %all-gather.7.cloned.1.call-done = bf16[4,512,512]{2,1,0:T(8,128)(2,1)} async-done(((bf16[1,512,512]{2,1,0:T(8,128)(2,1)}), bf16[4,512,512]{2,1,0:T(8,128)(2,1)}) %all-gather.7.cloned.1.call-update) | async-done | bytes 2097168 | tf_op jit(solution)/shard_map/all_gather | solution.py:62
  84.2 1.9 fusion.53
  87.4 5.1 %gather_fusion.5 = bf16[1024,512]{1,0:T(8,128)(2,1)} fusion(bf16[512,512]{1,0:T(8,128)(2,1)S(1)} %maximum_convert_fusion.3, s32[1024]{0:T(1024)S(1)} %fusion.49), kind=kCustom, calls=%fused_computation.2.clone | custom fusion | bytes 2101248 | tf_op jit(solution)/shard_map/jit(_take)/gather | solution.py:23
  92.5 1.4 broadcast_select_fusion.2
  95.1 4.6 %all-to-all-start.1 = ((bf16[8,128,512]{2,1,0:T(8,128)(2,1)}), bf16[8,128,512]{2,1,0:T(8,128)(2,1)}, u32[]{:S(2)}, u32[]{:S(2)}) async-start(bf16[8,128,512]{2,1,0:T(8,128)(2,1)} %broadcast_select_fusion.6), calls=%async_computation.1 | async-start | bytes 2097152 | tf_op jit(solution)/shard_map/all_to_all | solution.py:28
  99.7 2.5 fusion.47
  102.2 24.2 %all-to-all-done.1 = bf16[8,128,512]{2,1,0:T(8,128)(2,1)} async-done(((bf16[8,128,512]{2,1,0:T(8,128)(2,1)}), bf16[8,128,512]{2,1,0:T(8,128)(2,1)}, u32[]{:S(2)}, u32[]{:S(2)}) %all-to-all-start.1) | async-done | bytes 1048608 | tf_op jit(solution)/shard_map/all_to_all | solution.py:28
  126.4 2.5 pad_maximum_fusion.1
  128.9 13.2 %while.41 = (s32[]{:T(128)}, bf16[4,128,512]{2,1,0:T(8,128)(2,1)S(1)}, pred[4,4]{1,0:T(4,128)(4,1)S(1)}, bf16[4,4,128,128]{3,2,1,0:T(8,128)(2,1)}, s32[4,4]{1,0:...) while((s32[]{:T(128)}, bf16[4,128,512]{2,1,0:T(8,128)(2,1)S(1)}, pred[4,4]{1,0:T(4,128)(4,1)S(1)}, ...), condition=%wide.region_5.8_spmd, body=%wide.region_4.7_spmd.sunk | while | flops 67437592 | bytes 1972385 | solution.py:40
  129.0 2.0 gather_fusion.1
  132.2 2.0 gather_fusion.1
  134.3 1.2 fusion.79
  135.5 2.0 gather_fusion.1
  138.8 2.0 gather_fusion.1
  140.8 1.2 fusion.79
  142.1 1.9 fusion.54
  145.3 5.1 %gather_fusion.6 = bf16[1024,512]{1,0:T(8,128)(2,1)} fusion(bf16[512,512]{1,0:T(8,128)(2,1)S(1)} %maximum_convert_fusion.2, s32[1024]{0:T(1024)S(1)} %fusion.49), kind=kCustom, calls=%fused_computation.3.clone | custom fusion | bytes 2101248 | tf_op jit(solution)/shard_map/jit(_take)/gather | solution.py:23
  150.3 1.4 broadcast_select_fusion.1
  153.0 4.3 %all-to-all-start.2 = ((bf16[8,128,512]{2,1,0:T(8,128)(2,1)}), bf16[8,128,512]{2,1,0:T(8,128)(2,1)}, u32[]{:S(2)}, u32[]{:S(2)}) async-start(bf16[8,128,512]{2,1,0:T(8,128)(2,1)} %broadcast_select_fusion.5), calls=%async_computation.2 | async-start | bytes 2097152 | tf_op jit(solution)/shard_map/all_to_all | solution.py:28
  157.2 2.5 fusion.46
  159.7 24.1 %all-to-all-done.2 = bf16[8,128,512]{2,1,0:T(8,128)(2,1)} async-done(((bf16[8,128,512]{2,1,0:T(8,128)(2,1)}), bf16[8,128,512]{2,1,0:T(8,128)(2,1)}, u32[]{:S(2)}, u32[]{:S(2)}) %all-to-all-start.2) | async-done | bytes 1048608 | tf_op jit(solution)/shard_map/all_to_all | solution.py:28
  183.8 2.5 pad_maximum_fusion.2
  186.3 13.2 %while.42 = (s32[]{:T(128)}, bf16[4,128,512]{2,1,0:T(8,128)(2,1)S(1)}, pred[4,4]{1,0:T(4,128)(4,1)S(1)}, bf16[4,4,128,128]{3,2,1,0:T(8,128)(2,1)}, s32[4,4]{1,0:...) while((s32[]{:T(128)}, bf16[4,128,512]{2,1,0:T(8,128)(2,1)S(1)}, pred[4,4]{1,0:T(4,128)(4,1)S(1)}, ...), condition=%wide.region_9.12_spmd, body=%wide.region_8.11_spmd.sunk | while | flops 67437592 | bytes 1972385 | solution.py:40
  186.4 2.0 gather_fusion.2
  188.4 1.2 fusion.81
  189.7 2.0 gather_fusion.2
  193.0 2.0 gather_fusion.2
  196.2 2.0 gather_fusion.2
  198.3 1.2 fusion.81
  199.5 1.9 fusion.55
  202.7 5.1 %gather_fusion.7 = bf16[1024,512]{1,0:T(8,128)(2,1)} fusion(bf16[512,512]{1,0:T(8,128)(2,1)S(1)} %maximum_convert_fusion.1, s32[1024]{0:T(1024)S(1)} %fusion.49), kind=kCustom, calls=%fused_computation.4.clone | custom fusion | bytes 2101248 | tf_op jit(solution)/shard_map/jit(_take)/gather | solution.py:23
  207.8 1.4 broadcast_select_fusion
  210.4 4.2 %all-to-all-start.3 = ((bf16[8,128,512]{2,1,0:T(8,128)(2,1)}), bf16[8,128,512]{2,1,0:T(8,128)(2,1)}, u32[]{:S(2)}, u32[]{:S(2)}) async-start(bf16[8,128,512]{2,1,0:T(8,128)(2,1)} %broadcast_select_fusion.4), calls=%async_computation.3 | async-start | bytes 2097152 | tf_op jit(solution)/shard_map/all_to_all | solution.py:28
  214.7 2.5 fusion.64
  219.3 2.5 fusion.45
  221.8 19.4 %all-to-all-done.3 = bf16[8,128,512]{2,1,0:T(8,128)(2,1)} async-done(((bf16[8,128,512]{2,1,0:T(8,128)(2,1)}), bf16[8,128,512]{2,1,0:T(8,128)(2,1)}, u32[]{:S(2)}, u32[]{:S(2)}) %all-to-all-start.3) | async-done | bytes 1048608 | tf_op jit(solution)/shard_map/all_to_all | solution.py:28
  241.2 2.5 pad_maximum_fusion.3
  243.8 13.2 %while.43 = (s32[]{:T(128)}, bf16[4,128,512]{2,1,0:T(8,128)(2,1)S(1)}, pred[4,4]{1,0:T(4,128)(4,1)S(1)}, bf16[4,4,128,128]{3,2,1,0:T(8,128)(2,1)}, s32[4,4]{1,0:...) while((s32[]{:T(128)}, bf16[4,128,512]{2,1,0:T(8,128)(2,1)S(1)}, pred[4,4]{1,0:T(4,128)(4,1)S(1)}, ...), condition=%wide.region_13.16_spmd, body=%wide.region_12.15_spmd.sunk | while | flops 67437592 | bytes 1972385 | solution.py:40
  243.8 2.0 gather_fusion.3
  247.1 2.0 gather_fusion.3
  250.4 2.0 gather_fusion.3
  252.4 1.2 fusion.83
  253.7 2.0 gather_fusion.3
  256.9 1.9 fusion.56
  260.5 27.8 %all_to_all.32 = bf16[4,1,512,512]{3,2,1,0:T(8,128)(2,1)S(1)} all-to-all(bf16[4,1,512,512]{3,2,1,0:T(8,128)(2,1)S(1)} %maximum_bitcast_fusion), channel_id=1, replica_groups=mesh['segment'=4,'dom'=8] {'segment'}, dimensions={0} | all-to-all | bytes 4194304 | tf_op jit(solution)/shard_map/all_to_all | solution.py:84
  288.3 1.3 copy.49
  (122 shorter events, 27.5 us)
Async XLA Ops:
  6.5 1.6 copy-start
  6.5 63.0 %all-gather.5.cloned.1.call-start = ((), (), s32[]{:S(2)}) async-start(), calls=%async_computation.5 | async-start | bytes 2621440 | tf_op jit(solution)/shard_map/all_gather | solution.py:61
  16.1 8.4 %copy-start.10 = (bf16[1,512]{1,0:T(2,128)(2,1)S(1)}, bf16[1,512]{1,0:T(2,128)(2,1)}, u32[]{:S(2)}) copy-start(bf16[1,512]{1,0:T(2,128)(2,1)} %param.30) | copy-start | bytes 3076
  17.3 16.9 %copy-start.11 = (bf16[1,512]{1,0:T(2,128)(2,1)S(1)}, bf16[1,512]{1,0:T(2,128)(2,1)}, u32[]{:S(2)}) copy-start(bf16[1,512]{1,0:T(2,128)(2,1)} %param.31) | copy-start | bytes 3076
  17.3 33.2 %all-to-all-start = ((bf16[8,128,512]{2,1,0:T(8,128)(2,1)}), bf16[8,128,512]{2,1,0:T(8,128)(2,1)}, u32[]{:S(2)}, u32[]{:S(2)}) async-start(bf16[8,128,512]{2,1,0:T(8,128)(2,1)} %broadcast_select_fusion.7), calls=%async_computation | async-start | bytes 2097152 | tf_op jit(solution)/shard_map/all_to_all | solution.py:28
  23.8 60.4 %all-gather.7.cloned.1.call-start = ((), (), s32[]{:S(2)}) async-start(), calls=%async_computation.6 | async-start | bytes 2621440 | tf_op jit(solution)/shard_map/all_gather | solution.py:62
  69.5 14.7 %copy-start.6 = (bf16[4,128,512]{2,1,0:T(8,128)(2,1)S(1)}, bf16[4,128,512]{2,1,0:T(8,128)(2,1)}, u32[]{:S(2)}) copy-start(bf16[4,128,512]{2,1,0:T(8,128)(2,1)} %get-tuple-element.135) | copy-start | bytes 1572868
  86.1 1.0 copy-start.1
  95.1 31.3 %all-to-all-start.1 = ((bf16[8,128,512]{2,1,0:T(8,128)(2,1)}), bf16[8,128,512]{2,1,0:T(8,128)(2,1)}, u32[]{:S(2)}, u32[]{:S(2)}) async-start(bf16[8,128,512]{2,1,0:T(8,128)(2,1)} %broadcast_select_fusion.6), calls=%async_computation.1 | async-start | bytes 2097152 | tf_op jit(solution)/shard_map/all_to_all | solution.py:28
  144.0 1.0 copy-start.2
  153.0 30.8 %all-to-all-start.2 = ((bf16[8,128,512]{2,1,0:T(8,128)(2,1)}), bf16[8,128,512]{2,1,0:T(8,128)(2,1)}, u32[]{:S(2)}, u32[]{:S(2)}) async-start(bf16[8,128,512]{2,1,0:T(8,128)(2,1)} %broadcast_select_fusion.5), calls=%async_computation.2 | async-start | bytes 2097152 | tf_op jit(solution)/shard_map/all_to_all | solution.py:28
  201.4 1.0 copy-start.4
  210.4 30.8 %all-to-all-start.3 = ((bf16[8,128,512]{2,1,0:T(8,128)(2,1)}), bf16[8,128,512]{2,1,0:T(8,128)(2,1)}, u32[]{:S(2)}, u32[]{:S(2)}) async-start(bf16[8,128,512]{2,1,0:T(8,128)(2,1)} %broadcast_select_fusion.4), calls=%async_computation.3 | async-start | bytes 2097152 | tf_op jit(solution)/shard_map/all_to_all | solution.py:28
  214.7 2.5 copy-start.3
  214.7 3.6 %copy-start.5 = (f32[512,512]{1,0:T(8,128)S(1)}, f32[512,512]{1,0:T(8,128)}, u32[]{:S(2)}) copy-start(f32[512,512]{1,0:T(8,128)} %copy-done.4) | copy-start | bytes 3145732
  258.9 1.0 copy-start.7
  258.9 1.2 copy-start.8
  258.9 1.3 copy-start.9
Sparse Core Ops, SparseCore 0:
  9.2 37.9 all-gather.4
  49.0 35.1 all-gather.6
where the time goes:
time: 298 us; the launch traced here: 296 us
  waiting for transfers between devices  87.4 us (29%)
  local copies, waits for them, and re-layouts  61.9 us (21%)
  blocking collectives  44.2 us (15%)
  matrix products  39.7 us (13%)
  other arithmetic  29.3 us (10%)
  starting transfers between devices  19.6 us (7%)
  between operations  13.7 us (5%)
    all_to_all x4, waiting for transfers between devices, sage_layer(): lax.all_to_all(outgoing, 'dom', split_axis=0, concat_axis=0, tiled=True)  73.8 us
    gather x16, local copies, waits for them, and re-layouts, block_sum(): chosen = jnp.take(sources, block_index, axis=0)  31.8 us
    all_to_all x1, blocking collectives, per_device(): lax.all_to_all(dealt_out, 'segment', split_axis=0, concat_axis=1, tiled=T...  27.8 us
    dot_general x16, matrix products, block_sum(): jnp.einsum('kij,kjd->id', masked, chosen, preferred_element_type=jnp.floa...  22.2 us
    gather x4, local copies, waits for them, and re-layouts, sage_layer(): jnp.take(inputs, send_list.reshape(-1), axis=0)  20.3 us
    all_to_all x4, starting transfers between devices, sage_layer(): lax.all_to_all(outgoing, 'dom', split_axis=0, concat_axis=0, tiled=True)  19.6 us
    all_gather x1, waiting for transfers between devices, per_device(): lax.all_gather(w_neigh, 'segment', axis=0, tiled=True)  12.2 us
    concatenate x4, other arithmetic, sage_layer(): jnp.concatenate([inputs.reshape(block_count, tile_rows, feat_width), inco...  10 us
  transfers between devices with their start and end apart: 6, of which 5 were waited for; matrix products, arithmetic and copies ran while one was open for 16% of the time, Pallas kernels for 0%

commit v1 on v0

--- a/solution.py
+++ b/solution.py
@@ -2,6 +2,7 @@
 import jax.numpy as jnp
 from jax import lax
 from jax.sharding import PartitionSpec as P
+from jax.lax import axis_index, axis_size, ppermute
 
 norm_eps = 1e-05
 
@@ -25,7 +26,21 @@
     )
     row_live = lax.broadcasted_iota(jnp.int32, (peer_count, tile_rows), 1) < send_count[:, None]
     outgoing = jnp.where(row_live[:, :, None], picked, jnp.zeros_like(picked))
-    incoming = lax.all_to_all(outgoing, "dom", split_axis=0, concat_axis=0, tiled=True)
+    tile_out = axis_size("dom")
+    seen_now = axis_index("dom")
+    outcome_arr, back = (tile_out, seen_now)
+    z2 = outgoing.shape[0] // outcome_arr
+    r1 = jnp.roll(outgoing, -back * z2, 0)
+    step_out = lax.slice_in_dim(r1, 0, z2, axis=0)
+    bank = [step_out]
+    for ii in range(1, outcome_arr):
+        wide_out = lax.slice_in_dim(r1, ii * z2, (ii + 1) * z2, axis=0)
+        carry_in = ppermute(
+            wide_out, "dom", [(h, (h + ii) % outcome_arr) for h in range(outcome_arr)]
+        )
+        bank.append(carry_in)
+    latest = jnp.concatenate(bank[::-1], 0)
+    incoming = jnp.roll(latest, (back + 1) * bank[0].shape[0], 0)
     sources = jnp.concatenate(
         [inputs.reshape(block_count, tile_rows, feat_width), incoming], axis=0
     )

time: 298 us -> 258 us (0.87)
  local copies, waits for them, and re-layouts: 61.9 us -> 44.1 us
  waiting for transfers between devices: 87.4 us -> 71.6 us
  other arithmetic: 29.3 us -> 15.8 us
  starting transfers between devices: 19.6 us -> 28.3 us
    all_to_all x4 -> x0, waiting for transfers between devices: 73.8 us -> none  [sage_layer(): lax.all_to_all(outgoing, 'dom', split_axis=0, concat_axis=0, tiled=True)]
    ppermute x0 -> x28, waiting for transfers between devices: none -> 53.3 us  [sage_layer(): ppermute(wide_out, 'dom', [(h, (h + ii) % outcome_arr) for h in range(out...]
    ppermute x0 -> x28, starting transfers between devices: none -> 28.3 us  [sage_layer(): ppermute(wide_out, 'dom', [(h, (h + ii) % outcome_arr) for h in range(out...]
    gather x16, local copies, waits for them, and re-layouts: 31.8 us -> 9.29 us  [block_sum(): chosen = jnp.take(sources, block_index, axis=0)]
    all_to_all x4 -> x0, starting transfers between devices: 19.6 us -> none  [sage_layer(): lax.all_to_all(outgoing, 'dom', split_axis=0, concat_axis=0, tiled=True)]
    concatenate x4, other arithmetic: 10 us -> 0.56 us  [sage_layer(): jnp.concatenate([inputs.reshape(block_count, tile_rows, feat_width), inco...]
    unnamed x25 -> x71, local copies, waits for them, and re-layouts: 4.51 us -> 11.5 us
    all_gather x1, waiting for transfers between devices: 12.2 us -> 17.6 us  [per_device(): lax.all_gather(w_neigh, 'segment', axis=0, tiled=True)]
  transfers between devices with their start and end apart: 6 -> 30, of which waited for: 5 -> 10; matrix products, arithmetic and copies ran while one was open for 16% -> 16% of each run, Pallas kernels for 0% -> 0%
where the time goes in v1:
time: 258 us; the launch traced here: 257 us
  waiting for transfers between devices  71.6 us (28%)
  local copies, waits for them, and re-layouts  44.1 us (17%)
  blocking collectives  43.4 us (17%)
  matrix products  38.7 us (15%)
  starting transfers between devices  28.3 us (11%)
  other arithmetic  15.8 us (6%)
  between operations  14.2 us (6%)
    ppermute x28, waiting for transfers between devices, sage_layer(): ppermute(wide_out, 'dom', [(h, (h + ii) % outcome_arr) for h in range(out...  53.3 us
    ppermute x28, starting transfers between devices, sage_layer(): ppermute(wide_out, 'dom', [(h, (h + ii) % outcome_arr) for h in range(out...  28.3 us
    all_to_all x1, blocking collectives, per_device(): lax.all_to_all(dealt_out, 'segment', split_axis=0, concat_axis=1, tiled=T...  27 us
    dot_general x16, matrix products, block_sum(): jnp.einsum('kij,kjd->id', masked, chosen, preferred_element_type=jnp.floa...  22.1 us
    all_gather x1, waiting for transfers between devices, per_device(): lax.all_gather(w_neigh, 'segment', axis=0, tiled=True)  17.6 us
    gather x4, local copies, waits for them, and re-layouts, sage_layer(): jnp.take(inputs, send_list.reshape(-1), axis=0)  17 us
    unnamed x71, local copies, waits for them, and re-layouts  11.5 us
    gather x16, local copies, waits for them, and re-layouts, block_sum(): chosen = jnp.take(sources, block_index, axis=0)  9.29 us
  transfers between devices with their start and end apart: 30, of which 10 were waited for; matrix products, arithmetic and copies ran while one was open for 16% of the time, Pallas kernels for 0%

profile of v1, /device:TPU:0, one launch (start us, length us, event | category | flops | bytes accessed | tf_op | source)
XLA Modules:
  0.0 256.8 jit_solution(874917755869917481)
XLA Ops:
  8.2 5.1 %gather_fusion.4 = bf16[1024,512]{1,0:T(8,128)(2,1)} fusion(bf16[512,512]{1,0:T(8,128)(2,1)S(1)} %fusion.81, s32[1024]{0:T(1024)S(1)} %fusion.58), kind=kCustom, calls=%fused_computation.clone | custom fusion | bytes 2101248 | tf_op jit(solution)/shard_map/jit(_take)/gather | solution.py:24
  14.7 1.4 broadcast_select_fusion.3
  16.7 1.0 copy-done.2
  17.8 4.6 %collective-permute-start = (bf16[1,128,512]{2,1,0:T(8,128)(2,1)S(1)}, bf16[1,128,512]{2,1,0:T(8,128)(2,1)}, u32[]{:S(2)}, u32[]{:S(2)}) collective-permute-start(bf16[1,128,512]{2,1,0:T(8,128)(2,1)S(1)} %get-tuple-element.223), channel_id=1, source_target_pairs={{0,7},{1,0},{2,1},{3,2},{4,3},{5,4},{6,5},{7,6},{8,15},{9,8},{10,9... | collective-permute-start | bytes 393224 | tf_op jit(solution)/shard_map/ppermute | solution.py:38
  23.0 2.7 %collective-permute-start.3 = (bf16[1,128,512]{2,1,0:T(8,128)(2,1)S(1)}, bf16[1,128,512]{2,1,0:T(8,128)(2,1)}, u32[]{:S(2)}, u32[]{:S(2)}) collective-permute-start(bf16[1,128,512]{2,1,0:T(8,128)(2,1)S(1)} %get-tuple-element.220), channel_id=1, source_target_pairs={{0,4},{1,5},{2,6},{3,7},{4,0},{5,1},{6,2},{7,3},{8,12},{9,13},{10,... | collective-permute-start | bytes 393224 | tf_op jit(solution)/shard_map/ppermute | solution.py:38
  27.0 8.1 %all-gather = bf16[4,1,512]{2,1,0:T(2,128)(2,1)S(1)} all-gather(bf16[1,1,512]{2,1,0:T(2,128)(2,1)S(1)} %bitcast.205), channel_id=1, replica_groups=mesh['segment'=4,'dom'=8] {'segment'}, dimensions={0}, use_global_device_ids=true | all-gather | bytes 5120 | tf_op jit(solution)/shard_map/all_gather | solution.py:78
  35.7 8.4 %all-gather.1 = bf16[4,1,512]{2,1,0:T(2,128)(2,1)S(1)} all-gather(bf16[1,1,512]{2,1,0:T(2,128)(2,1)} %bitcast.206), channel_id=1, replica_groups=mesh['segment'=4,'dom'=8] {'segment'}, dimensions={0}, use_global_device_ids=true | all-gather | bytes 5120 | tf_op jit(solution)/shard_map/all_gather | solution.py:79
  44.7 1.9 dynamic-slice_bitcast_fusion.4
  49.0 0.9 constant_dynamic-update-slice_fusion.5
  49.9 0.9 constant_dynamic-update-slice_fusion.4
  50.8 0.9 constant_dynamic-update-slice_fusion.3
  52.7 1.7 collective-permute-done.5
  54.4 1.1 collective-permute-done.6
  55.5 0.9 slice_dynamic-update-slice_fusion.3
  57.5 7.5 %while.40 = (s32[]{:T(128)}, bf16[4,128,512]{2,1,0:T(8,128)(2,1)S(1)}, pred[4,4]{1,0:T(4,128)(4,1)S(1)}, bf16[4,4,128,128]{3,2,1,0:T(8,128)(2,1)}, s32[4,4]{1,0:...) while((s32[]{:T(128)}, bf16[4,128,512]{2,1,0:T(8,128)(2,1)S(1)}, pred[4,4]{1,0:T(4,128)(4,1)S(1)}, ...), condition=%wide.region_1.5_spmd, body=%wide.region_0.4_spmd.sunk | while | flops 67437592 | bytes 1972385 | solution.py:55
  58.1 1.2 fusion.91
  60.0 1.2 fusion.91
  61.9 1.2 fusion.91
  63.7 1.2 fusion.91
  65.0 1.6 fusion.56
  66.7 17.6 %all-gather.7.cloned.1.call-done = bf16[4,512,512]{2,1,0:T(8,128)(2,1)} async-done(((bf16[1,512,512]{2,1,0:T(8,128)(2,1)}), bf16[4,512,512]{2,1,0:T(8,128)(2,1)}) %all-gather.7.cloned.1.call-update) | async-done | bytes 2097168 | tf_op jit(solution)/shard_map/all_gather | solution.py:77
  84.2 1.7 fusion.67
  86.5 4.0 %gather_fusion.5 = bf16[1024,512]{1,0:T(8,128)(2,1)S(1)} fusion(bf16[512,512]{1,0:T(8,128)(2,1)S(1)} %maximum_convert_fusion.3, s32[1024]{0:T(1024)S(1)} %fusion.58), kind=kCustom, calls=%fused_computation.2.clone | custom fusion | bytes 2101248 | tf_op jit(solution)/shard_map/jit(_take)/gather | solution.py:24
  91.8 2.7 %collective-permute-start.7 = (bf16[1,128,512]{2,1,0:T(8,128)(2,1)S(1)}, bf16[1,128,512]{2,1,0:T(8,128)(2,1)S(1)}, u32[]{:S(2)}, u32[]{:S(2)}) collective-permute-start(bf16[1,128,512]{2,1,0:T(8,128)(2,1)S(1)} %get-tuple-element.216), channel_id=1, source_target_pairs={{0,7},{1,0},{2,1},{3,2},{4,3},{5,4},{6,5},{7,6},{8,15},{9,8},{10,9... | collective-permute-start | bytes 393224 | tf_op jit(solution)/shard_map/ppermute | solution.py:38
  95.3 2.4 fusion.55
  97.7 1.1 fusion.78
  98.8 2.7 %collective-permute-start.10 = (bf16[1,128,512]{2,1,0:T(8,128)(2,1)S(1)}, bf16[1,128,512]{2,1,0:T(8,128)(2,1)S(1)}, u32[]{:S(2)}, u32[]{:S(2)}) collective-permute-start(bf16[1,128,512]{2,1,0:T(8,128)(2,1)S(1)} %get-tuple-element.213), channel_id=1, source_target_pairs={{0,4},{1,5},{2,6},{3,7},{4,0},{5,1},{6,2},{7,3},{8,12},{9,13},{10,... | collective-permute-start | bytes 393224 | tf_op jit(solution)/shard_map/ppermute | solution.py:38
  103.3 15.7 %collective-permute-done.10 = bf16[1,128,512]{2,1,0:T(8,128)(2,1)S(1)} collective-permute-done((bf16[1,128,512]{2,1,0:T(8,128)(2,1)S(1)}, bf16[1,128,512]{2,1,0:T(8,128)(2,1)S(1)}, u32[]{:S(2)}, u32[]{:S(2)}) %collective-permute-start.10) | collective-permute-done | bytes 131104 | tf_op jit(solution)/shard_map/ppermute | solution.py:38
  119.0 1.1 collective-permute-done.11
  120.8 7.5 %while.41 = (s32[]{:T(128)}, bf16[4,128,512]{2,1,0:T(8,128)(2,1)S(1)}, pred[4,4]{1,0:T(4,128)(4,1)S(1)}, bf16[4,4,128,128]{3,2,1,0:T(8,128)(2,1)}, s32[4,4]{1,0:...) while((s32[]{:T(128)}, bf16[4,128,512]{2,1,0:T(8,128)(2,1)S(1)}, pred[4,4]{1,0:T(4,128)(4,1)S(1)}, ...), condition=%wide.region_5.9_spmd, body=%wide.region_4.8_spmd.sunk | while | flops 67437592 | bytes 1972385 | solution.py:55
  121.4 1.2 fusion.93
  123.3 1.2 fusion.93
  125.2 1.2 fusion.93
  127.0 1.2 fusion.93
  129.1 2.1 fusion.68
  131.7 4.0 %gather_fusion.6 = bf16[1024,512]{1,0:T(8,128)(2,1)S(1)} fusion(bf16[512,512]{1,0:T(8,128)(2,1)S(1)} %maximum_convert_fusion.2, s32[1024]{0:T(1024)S(1)} %fusion.58), kind=kCustom, calls=%fused_computation.3.clone | custom fusion | bytes 2101248 | tf_op jit(solution)/shard_map/jit(_take)/gather | solution.py:24
  137.4 2.4 fusion.54
  139.8 1.1 fusion.79
  141.6 1.6 collective-permute-start.17
  143.2 2.7 %collective-permute-start.19 = (bf16[1,128,512]{2,1,0:T(8,128)(2,1)S(1)}, bf16[1,128,512]{2,1,0:T(8,128)(2,1)S(1)}, u32[]{:S(2)}, u32[]{:S(2)}) collective-permute-start(bf16[1,128,512]{2,1,0:T(8,128)(2,1)S(1)} %get-tuple-element.204), channel_id=1, source_target_pairs={{0,2},{1,3},{2,4},{3,5},{4,6},{5,7},{6,0},{7,1},{8,10},{9,11},{10,... | collective-permute-start | bytes 393224 | tf_op jit(solution)/shard_map/ppermute | solution.py:38
  146.4 15.2 %collective-permute-done.17 = bf16[1,128,512]{2,1,0:T(8,128)(2,1)S(1)} collective-permute-done((bf16[1,128,512]{2,1,0:T(8,128)(2,1)S(1)}, bf16[1,128,512]{2,1,0:T(8,128)(2,1)S(1)}, u32[]{:S(2)}, u32[]{:S(2)}) %collective-permute-start.17) | collective-permute-done | bytes 131104 | tf_op jit(solution)/shard_map/ppermute | solution.py:38
  161.6 1.3 collective-permute-done.18
  163.6 7.5 %while.42 = (s32[]{:T(128)}, bf16[4,128,512]{2,1,0:T(8,128)(2,1)S(1)}, pred[4,4]{1,0:T(4,128)(4,1)S(1)}, bf16[4,4,128,128]{3,2,1,0:T(8,128)(2,1)}, s32[4,4]{1,0:...) while((s32[]{:T(128)}, bf16[4,128,512]{2,1,0:T(8,128)(2,1)S(1)}, pred[4,4]{1,0:T(4,128)(4,1)S(1)}, ...), condition=%wide.region_9.13_spmd, body=%wide.region_8.12_spmd.sunk | while | flops 67437592 | bytes 1972385 | solution.py:55
  164.3 1.2 fusion.95
  166.2 1.2 fusion.95
  168.1 1.2 fusion.95
  169.9 1.2 fusion.95
  172.0 2.1 fusion.69
  174.6 4.0 %gather_fusion.7 = bf16[1024,512]{1,0:T(8,128)(2,1)S(1)} fusion(bf16[512,512]{1,0:T(8,128)(2,1)S(1)} %maximum_convert_fusion.1, s32[1024]{0:T(1024)S(1)} %fusion.58), kind=kCustom, calls=%fused_computation.4.clone | custom fusion | bytes 2101248 | tf_op jit(solution)/shard_map/jit(_take)/gather | solution.py:24
  180.2 2.4 fusion.53
  182.7 1.1 fusion.80
  184.4 1.7 collective-permute-start.24
  186.3 2.4 collective-permute-start.26
  189.0 15.5 %collective-permute-done.24 = bf16[1,128,512]{2,1,0:T(8,128)(2,1)S(1)} collective-permute-done((bf16[1,128,512]{2,1,0:T(8,128)(2,1)S(1)}, bf16[1,128,512]{2,1,0:T(8,128)(2,1)S(1)}, u32[]{:S(2)}, u32[]{:S(2)}) %collective-permute-start.24) | collective-permute-done | bytes 131104 | tf_op jit(solution)/shard_map/ppermute | solution.py:38
  204.5 1.3 collective-permute-done.25
  207.3 10.0 %while.43 = (s32[]{:T(128)}, bf16[4,128,512]{2,1,0:T(8,128)(2,1)}, pred[4,4]{1,0:T(4,128)(4,1)S(1)}, bf16[4,4,128,128]{3,2,1,0:T(8,128)(2,1)}, s32[4,4]{1,0:T(4,...) while((s32[]{:T(128)}, bf16[4,128,512]{2,1,0:T(8,128)(2,1)}, pred[4,4]{1,0:T(4,128)(4,1)S(1)}, ...), condition=%wide.region_13.17_spmd, body=%wide.region_12.16_spmd.sunk | while | flops 67437592 | bytes 1971369 | solution.py:55
  207.9 1.9 fusion.97
  210.4 1.9 fusion.97
  212.9 1.9 fusion.97
  215.4 1.9 fusion.97
  217.3 1.7 fusion.70
  220.7 27.0 %all_to_all.12 = bf16[4,1,512,512]{3,2,1,0:T(8,128)(2,1)S(1)} all-to-all(bf16[4,1,512,512]{3,2,1,0:T(8,128)(2,1)S(1)} %maximum_bitcast_fusion), channel_id=1, replica_groups=mesh['segment'=4,'dom'=8] {'segment'}, dimensions={0} | all-to-all | bytes 4194304 | tf_op jit(solution)/shard_map/all_to_all | solution.py:99
  247.6 1.3 copy.77
  248.9 1.0 copy-done.1
  (232 shorter events, 37.7 us)
Async XLA Ops:
  6.5 1.6 copy-start
  6.5 58.5 %all-gather.5.cloned.1.call-start = ((), (), s32[]{:S(2)}) async-start(), calls=%async_computation.1 | async-start | bytes 2621440 | tf_op jit(solution)/shard_map/all_gather | solution.py:76
  7.3 77.0 %all-gather.7.cloned.1.call-start = ((), (), s32[]{:S(2)}) async-start(), calls=%async_computation.2 | async-start | bytes 2621440 | tf_op jit(solution)/shard_map/all_gather | solution.py:77
  14.7 1.7 copy-start.15
  16.7 1.0 copy-start.2
  17.7 9.3 %copy-start.19 = (bf16[1,512]{1,0:T(2,128)(2,1)S(1)}, bf16[1,512]{1,0:T(2,128)(2,1)}, u32[]{:S(2)}) copy-start(bf16[1,512]{1,0:T(2,128)(2,1)} %param.32) | copy-start | bytes 3076
  17.8 29.5 %collective-permute-start = (bf16[1,128,512]{2,1,0:T(8,128)(2,1)S(1)}, bf16[1,128,512]{2,1,0:T(8,128)(2,1)}, u32[]{:S(2)}, u32[]{:S(2)}) collective-permute-start(bf16[1,128,512]{2,1,0:T(8,128)(2,1)S(1)} %get-tuple-element.223), channel_id=1, source_target_pairs={{0,7},{1,0},{2,1},{3,2},{4,3},{5,4},{6,5},{7,6},{8,15},{9,8},{10,9... | collective-permute-start | bytes 393224 | tf_op jit(solution)/shard_map/ppermute | solution.py:38
  22.3 26.6 %collective-permute-start.1 = (bf16[1,128,512]{2,1,0:T(8,128)(2,1)S(1)}, bf16[1,128,512]{2,1,0:T(8,128)(2,1)}, u32[]{:S(2)}, u32[]{:S(2)}) collective-permute-start(bf16[1,128,512]{2,1,0:T(8,128)(2,1)S(1)} %get-tuple-element.222), channel_id=1, source_target_pairs={{0,6},{1,7},{2,0},{3,1},{4,2},{5,3},{6,4},{7,5},{8,14},{9,15},{10,... | collective-permute-start | bytes 393224 | tf_op jit(solution)/shard_map/ppermute | solution.py:38
  23.0 26.9 %collective-permute-start.2 = (bf16[1,128,512]{2,1,0:T(8,128)(2,1)S(1)}, bf16[1,128,512]{2,1,0:T(8,128)(2,1)}, u32[]{:S(2)}, u32[]{:S(2)}) collective-permute-start(bf16[1,128,512]{2,1,0:T(8,128)(2,1)S(1)} %get-tuple-element.221), channel_id=1, source_target_pairs={{0,5},{1,6},{2,7},{3,0},{4,1},{5,2},{6,3},{7,4},{8,13},{9,14},{10,... | collective-permute-start | bytes 393224 | tf_op jit(solution)/shard_map/ppermute | solution.py:38
  23.0 27.9 %collective-permute-start.3 = (bf16[1,128,512]{2,1,0:T(8,128)(2,1)S(1)}, bf16[1,128,512]{2,1,0:T(8,128)(2,1)}, u32[]{:S(2)}, u32[]{:S(2)}) collective-permute-start(bf16[1,128,512]{2,1,0:T(8,128)(2,1)S(1)} %get-tuple-element.220), channel_id=1, source_target_pairs={{0,4},{1,5},{2,6},{3,7},{4,0},{5,1},{6,2},{7,3},{8,12},{9,13},{10,... | collective-permute-start | bytes 393224 | tf_op jit(solution)/shard_map/ppermute | solution.py:38
  25.7 26.1 %collective-permute-start.4 = (bf16[1,128,512]{2,1,0:T(8,128)(2,1)S(1)}, bf16[1,128,512]{2,1,0:T(8,128)(2,1)}, u32[]{:S(2)}, u32[]{:S(2)}) collective-permute-start(bf16[1,128,512]{2,1,0:T(8,128)(2,1)S(1)} %get-tuple-element.219), channel_id=1, source_target_pairs={{0,3},{1,4},{2,5},{3,6},{4,7},{5,0},{6,1},{7,2},{8,11},{9,12},{10,... | collective-permute-start | bytes 393224 | tf_op jit(solution)/shard_map/ppermute | solution.py:38
  47.3 7.1 %collective-permute-start.5 = (bf16[1,128,512]{2,1,0:T(8,128)(2,1)S(1)}, bf16[1,128,512]{2,1,0:T(8,128)(2,1)S(1)}, u32[]{:S(2)}, u32[]{:S(2)}) collective-permute-start(bf16[1,128,512]{2,1,0:T(8,128)(2,1)S(1)} %get-tuple-element.218), channel_id=1, source_target_pairs={{0,2},{1,3},{2,4},{3,5},{4,6},{5,7},{6,0},{7,1},{8,10},{9,11},{10,... | collective-permute-start | bytes 393224 | tf_op jit(solution)/shard_map/ppermute | solution.py:38
  48.9 6.6 %collective-permute-start.6 = (bf16[1,128,512]{2,1,0:T(8,128)(2,1)S(1)}, bf16[1,128,512]{2,1,0:T(8,128)(2,1)S(1)}, u32[]{:S(2)}, u32[]{:S(2)}) collective-permute-start(bf16[1,128,512]{2,1,0:T(8,128)(2,1)S(1)} %get-tuple-element.217), channel_id=1, source_target_pairs={{0,1},{1,2},{2,3},{3,4},{4,5},{5,6},{6,7},{7,0},{8,9},{9,10},{10,1... | collective-permute-start | bytes 393224 | tf_op jit(solution)/shard_map/ppermute | solution.py:38
  56.8 0.6 copy-start.20
  65.0 19.3 %copy-start.4 = (bf16[4,128,512]{2,1,0:T(8,128)(2,1)}, bf16[4,128,512]{2,1,0:T(8,128)(2,1)S(1)}, u32[]{:S(2)}) copy-start(bf16[4,128,512]{2,1,0:T(8,128)(2,1)S(1)} %get-tuple-element.136) | copy-start | bytes 1572868
  84.2 2.0 copy-start.13
  84.2 2.0 copy-start.14
  90.5 0.6 copy-start.16
  91.8 9.7 %collective-permute-start.7 = (bf16[1,128,512]{2,1,0:T(8,128)(2,1)S(1)}, bf16[1,128,512]{2,1,0:T(8,128)(2,1)S(1)}, u32[]{:S(2)}, u32[]{:S(2)}) collective-permute-start(bf16[1,128,512]{2,1,0:T(8,128)(2,1)S(1)} %get-tuple-element.216), channel_id=1, source_target_pairs={{0,7},{1,0},{2,1},{3,2},{4,3},{5,4},{6,5},{7,6},{8,15},{9,8},{10,9... | collective-permute-start | bytes 393224 | tf_op jit(solution)/shard_map/ppermute | solution.py:38
  94.5 7.8 %collective-permute-start.8 = (bf16[1,128,512]{2,1,0:T(8,128)(2,1)S(1)}, bf16[1,128,512]{2,1,0:T(8,128)(2,1)S(1)}, u32[]{:S(2)}, u32[]{:S(2)}) collective-permute-start(bf16[1,128,512]{2,1,0:T(8,128)(2,1)S(1)} %get-tuple-element.215), channel_id=1, source_target_pairs={{0,6},{1,7},{2,0},{3,1},{4,2},{5,3},{6,4},{7,5},{8,14},{9,15},{10,... | collective-permute-start | bytes 393224 | tf_op jit(solution)/shard_map/ppermute | solution.py:38
  98.8 4.4 %collective-permute-start.9 = (bf16[1,128,512]{2,1,0:T(8,128)(2,1)S(1)}, bf16[1,128,512]{2,1,0:T(8,128)(2,1)S(1)}, u32[]{:S(2)}, u32[]{:S(2)}) collective-permute-start(bf16[1,128,512]{2,1,0:T(8,128)(2,1)S(1)} %get-tuple-element.214), channel_id=1, source_target_pairs={{0,5},{1,6},{2,7},{3,0},{4,1},{5,2},{6,3},{7,4},{8,13},{9,14},{10,... | collective-permute-start | bytes 393224 | tf_op jit(solution)/shard_map/ppermute | solution.py:38
  98.8 20.1 %collective-permute-start.10 = (bf16[1,128,512]{2,1,0:T(8,128)(2,1)S(1)}, bf16[1,128,512]{2,1,0:T(8,128)(2,1)S(1)}, u32[]{:S(2)}, u32[]{:S(2)}) collective-permute-start(bf16[1,128,512]{2,1,0:T(8,128)(2,1)S(1)} %get-tuple-element.213), channel_id=1, source_target_pairs={{0,4},{1,5},{2,6},{3,7},{4,0},{5,1},{6,2},{7,3},{8,12},{9,13},{10,... | collective-permute-start | bytes 393224 | tf_op jit(solution)/shard_map/ppermute | solution.py:38
  101.5 18.6 %collective-permute-start.11 = (bf16[1,128,512]{2,1,0:T(8,128)(2,1)S(1)}, bf16[1,128,512]{2,1,0:T(8,128)(2,1)S(1)}, u32[]{:S(2)}, u32[]{:S(2)}) collective-permute-start(bf16[1,128,512]{2,1,0:T(8,128)(2,1)S(1)} %get-tuple-element.212), channel_id=1, source_target_pairs={{0,3},{1,4},{2,5},{3,6},{4,7},{5,0},{6,1},{7,2},{8,11},{9,12},{10,... | collective-permute-start | bytes 393224 | tf_op jit(solution)/shard_map/ppermute | solution.py:38
  101.5 18.6 %collective-permute-start.12 = (bf16[1,128,512]{2,1,0:T(8,128)(2,1)S(1)}, bf16[1,128,512]{2,1,0:T(8,128)(2,1)S(1)}, u32[]{:S(2)}, u32[]{:S(2)}) collective-permute-start(bf16[1,128,512]{2,1,0:T(8,128)(2,1)S(1)} %get-tuple-element.211), channel_id=1, source_target_pairs={{0,2},{1,3},{2,4},{3,5},{4,6},{5,7},{6,0},{7,1},{8,10},{9,11},{10,... | collective-permute-start | bytes 393224 | tf_op jit(solution)/shard_map/ppermute | solution.py:38
  102.3 17.8 %collective-permute-start.13 = (bf16[1,128,512]{2,1,0:T(8,128)(2,1)S(1)}, bf16[1,128,512]{2,1,0:T(8,128)(2,1)S(1)}, u32[]{:S(2)}, u32[]{:S(2)}) collective-permute-start(bf16[1,128,512]{2,1,0:T(8,128)(2,1)S(1)} %get-tuple-element.210), channel_id=1, source_target_pairs={{0,1},{1,2},{2,3},{3,4},{4,5},{5,6},{6,7},{7,0},{8,9},{9,10},{10,1... | collective-permute-start | bytes 393224 | tf_op jit(solution)/shard_map/ppermute | solution.py:38
  128.3 0.8 copy-start.5
  129.1 2.4 copy-start.11
  129.1 2.4 copy-start.12
  136.6 6.6 %collective-permute-start.14 = (bf16[1,128,512]{2,1,0:T(8,128)(2,1)S(1)}, bf16[1,128,512]{2,1,0:T(8,128)(2,1)S(1)}, u32[]{:S(2)}, u32[]{:S(2)}) collective-permute-start(bf16[1,128,512]{2,1,0:T(8,128)(2,1)S(1)} %get-tuple-element.209), channel_id=1, source_target_pairs={{0,7},{1,0},{2,1},{3,2},{4,3},{5,4},{6,5},{7,6},{8,15},{9,8},{10,9... | collective-permute-start | bytes 393224 | tf_op jit(solution)/shard_map/ppermute | solution.py:38
  136.7 9.3 %collective-permute-start.15 = (bf16[1,128,512]{2,1,0:T(8,128)(2,1)S(1)}, bf16[1,128,512]{2,1,0:T(8,128)(2,1)S(1)}, u32[]{:S(2)}, u32[]{:S(2)}) collective-permute-start(bf16[1,128,512]{2,1,0:T(8,128)(2,1)S(1)} %get-tuple-element.208), channel_id=1, source_target_pairs={{0,6},{1,7},{2,0},{3,1},{4,2},{5,3},{6,4},{7,5},{8,14},{9,15},{10,... | collective-permute-start | bytes 393224 | tf_op jit(solution)/shard_map/ppermute | solution.py:38
  140.9 5.5 %collective-permute-start.16 = (bf16[1,128,512]{2,1,0:T(8,128)(2,1)S(1)}, bf16[1,128,512]{2,1,0:T(8,128)(2,1)S(1)}, u32[]{:S(2)}, u32[]{:S(2)}) collective-permute-start(bf16[1,128,512]{2,1,0:T(8,128)(2,1)S(1)} %get-tuple-element.207), channel_id=1, source_target_pairs={{0,5},{1,6},{2,7},{3,0},{4,1},{5,2},{6,3},{7,4},{8,13},{9,14},{10,... | collective-permute-start | bytes 393224 | tf_op jit(solution)/shard_map/ppermute | solution.py:38
  141.6 20.0 %collective-permute-start.17 = (bf16[1,128,512]{2,1,0:T(8,128)(2,1)S(1)}, bf16[1,128,512]{2,1,0:T(8,128)(2,1)S(1)}, u32[]{:S(2)}, u32[]{:S(2)}) collective-permute-start(bf16[1,128,512]{2,1,0:T(8,128)(2,1)S(1)} %get-tuple-element.206), channel_id=1, source_target_pairs={{0,4},{1,5},{2,6},{3,7},{4,0},{5,1},{6,2},{7,3},{8,12},{9,13},{10,... | collective-permute-start | bytes 393224 | tf_op jit(solution)/shard_map/ppermute | solution.py:38
  143.2 19.7 %collective-permute-start.18 = (bf16[1,128,512]{2,1,0:T(8,128)(2,1)S(1)}, bf16[1,128,512]{2,1,0:T(8,128)(2,1)S(1)}, u32[]{:S(2)}, u32[]{:S(2)}) collective-permute-start(bf16[1,128,512]{2,1,0:T(8,128)(2,1)S(1)} %get-tuple-element.205), channel_id=1, source_target_pairs={{0,3},{1,4},{2,5},{3,6},{4,7},{5,0},{6,1},{7,2},{8,11},{9,12},{10,... | collective-permute-start | bytes 393224 | tf_op jit(solution)/shard_map/ppermute | solution.py:38
  143.2 19.7 %collective-permute-start.19 = (bf16[1,128,512]{2,1,0:T(8,128)(2,1)S(1)}, bf16[1,128,512]{2,1,0:T(8,128)(2,1)S(1)}, u32[]{:S(2)}, u32[]{:S(2)}) collective-permute-start(bf16[1,128,512]{2,1,0:T(8,128)(2,1)S(1)} %get-tuple-element.204), channel_id=1, source_target_pairs={{0,2},{1,3},{2,4},{3,5},{4,6},{5,7},{6,0},{7,1},{8,10},{9,11},{10,... | collective-permute-start | bytes 393224 | tf_op jit(solution)/shard_map/ppermute | solution.py:38
  146.0 17.0 %collective-permute-start.20 = (bf16[1,128,512]{2,1,0:T(8,128)(2,1)S(1)}, bf16[1,128,512]{2,1,0:T(8,128)(2,1)S(1)}, u32[]{:S(2)}, u32[]{:S(2)}) collective-permute-start(bf16[1,128,512]{2,1,0:T(8,128)(2,1)S(1)} %get-tuple-element.203), channel_id=1, source_target_pairs={{0,1},{1,2},{2,3},{3,4},{4,5},{5,6},{6,7},{7,0},{8,9},{9,10},{10,1... | collective-permute-start | bytes 393224 | tf_op jit(solution)/shard_map/ppermute | solution.py:38
  171.2 0.8 copy-start.6
  172.0 2.3 copy-start.10
  179.5 6.8 %collective-permute-start.21 = (bf16[1,128,512]{2,1,0:T(8,128)(2,1)S(1)}, bf16[1,128,512]{2,1,0:T(8,128)(2,1)S(1)}, u32[]{:S(2)}, u32[]{:S(2)}) collective-permute-start(bf16[1,128,512]{2,1,0:T(8,128)(2,1)S(1)} %get-tuple-element.202), channel_id=1, source_target_pairs={{0,7},{1,0},{2,1},{3,2},{4,3},{5,4},{6,5},{7,6},{8,15},{9,8},{10,9... | collective-permute-start | bytes 393224 | tf_op jit(solution)/shard_map/ppermute | solution.py:38
  179.5 9.2 %collective-permute-start.22 = (bf16[1,128,512]{2,1,0:T(8,128)(2,1)S(1)}, bf16[1,128,512]{2,1,0:T(8,128)(2,1)S(1)}, u32[]{:S(2)}, u32[]{:S(2)}) collective-permute-start(bf16[1,128,512]{2,1,0:T(8,128)(2,1)S(1)} %get-tuple-element.201), channel_id=1, source_target_pairs={{0,6},{1,7},{2,0},{3,1},{4,2},{5,3},{6,4},{7,5},{8,14},{9,15},{10,... | collective-permute-start | bytes 393224 | tf_op jit(solution)/shard_map/ppermute | solution.py:38
  183.8 5.2 %collective-permute-start.23 = (bf16[1,128,512]{2,1,0:T(8,128)(2,1)S(1)}, bf16[1,128,512]{2,1,0:T(8,128)(2,1)S(1)}, u32[]{:S(2)}, u32[]{:S(2)}) collective-permute-start(bf16[1,128,512]{2,1,0:T(8,128)(2,1)S(1)} %get-tuple-element.200), channel_id=1, source_target_pairs={{0,5},{1,6},{2,7},{3,0},{4,1},{5,2},{6,3},{7,4},{8,13},{9,14},{10,... | collective-permute-start | bytes 393224 | tf_op jit(solution)/shard_map/ppermute | solution.py:38
  184.4 20.1 %collective-permute-start.24 = (bf16[1,128,512]{2,1,0:T(8,128)(2,1)S(1)}, bf16[1,128,512]{2,1,0:T(8,128)(2,1)S(1)}, u32[]{:S(2)}, u32[]{:S(2)}) collective-permute-start(bf16[1,128,512]{2,1,0:T(8,128)(2,1)S(1)} %get-tuple-element.199), channel_id=1, source_target_pairs={{0,4},{1,5},{2,6},{3,7},{4,0},{5,1},{6,2},{7,3},{8,12},{9,13},{10,... | collective-permute-start | bytes 393224 | tf_op jit(solution)/shard_map/ppermute | solution.py:38
  186.1 19.7 %collective-permute-start.25 = (bf16[1,128,512]{2,1,0:T(8,128)(2,1)S(1)}, bf16[1,128,512]{2,1,0:T(8,128)(2,1)S(1)}, u32[]{:S(2)}, u32[]{:S(2)}) collective-permute-start(bf16[1,128,512]{2,1,0:T(8,128)(2,1)S(1)} %get-tuple-element.198), channel_id=1, source_target_pairs={{0,3},{1,4},{2,5},{3,6},{4,7},{5,0},{6,1},{7,2},{8,11},{9,12},{10,... | collective-permute-start | bytes 393224 | tf_op jit(solution)/shard_map/ppermute | solution.py:38
  186.3 19.6 %collective-permute-start.26 = (bf16[1,128,512]{2,1,0:T(8,128)(2,1)S(1)}, bf16[1,128,512]{2,1,0:T(8,128)(2,1)S(1)}, u32[]{:S(2)}, u32[]{:S(2)}) collective-permute-start(bf16[1,128,512]{2,1,0:T(8,128)(2,1)S(1)} %get-tuple-element.197), channel_id=1, source_target_pairs={{0,2},{1,3},{2,4},{3,5},{4,6},{5,7},{6,0},{7,1},{8,10},{9,11},{10,... | collective-permute-start | bytes 393224 | tf_op jit(solution)/shard_map/ppermute | solution.py:38
  188.7 17.1 %collective-permute-start.27 = (bf16[1,128,512]{2,1,0:T(8,128)(2,1)S(1)}, bf16[1,128,512]{2,1,0:T(8,128)(2,1)S(1)}, u32[]{:S(2)}, u32[]{:S(2)}) collective-permute-start(bf16[1,128,512]{2,1,0:T(8,128)(2,1)S(1)} %get-tuple-element.196), channel_id=1, source_target_pairs={{0,1},{1,2},{2,3},{3,4},{4,5},{5,6},{6,7},{7,0},{8,9},{9,10},{10,1... | collective-permute-start | bytes 393224 | tf_op jit(solution)/shard_map/ppermute | solution.py:38
  207.3 10.0 %copy-start.3 = (f32[512,512]{1,0:T(8,128)S(1)}, f32[512,512]{1,0:T(8,128)}, u32[]{:S(2)}) copy-start(f32[512,512]{1,0:T(8,128)} %fusion.53) | copy-start | bytes 3145732
  217.3 2.0 copy-start.17
  217.3 2.0 copy-start.18
  219.0 1.0 copy-start.7
  219.0 1.2 copy-start.8
  219.0 1.3 copy-start.9
  247.6 2.3 copy-start.1
Sparse Core Ops, SparseCore 0:
  9.2 37.9 all-gather.4
  49.0 35.1 all-gather.6
